TPU v7x, 32 devices: a whole 2x2x4 slice. The times are simulated.
32 devices in a mesh: section: 16 (over z, y, core), dp: 2 (over x).
Axes of the slice: x: 2, y: 2, z: 4, core: 2. Of those that a mesh axis runs over, the one named last changes fastest.
Arguments:
- section_states: bfloat16 [16, 4, 2, 16, 16, 512], P('section', None, 'dp'), may hold values from -6 to 6
- conv_kernels: bfloat16 [16, 2, 1152, 512], P('section'), may hold values from -0.1875 to 0.1875
- top_feed: bfloat16 [3, 4, 2, 16, 16, 512], P(None, None, 'dp'), may hold values from -6 to 6
Outputs:
- final_states: bfloat16 [16, 4, 2, 16, 16, 512], P('section', None, 'dp')
- kernel_grads: float32 [16, 2, 1152, 512], P('section', None, 'dp')
All inputs are finite; a program needn't handle non-finite values.
Results may differ from a plain program's by a relative error of at most 0.024.
Values may be sent and summed in bfloat16 or wider, within the bound.
A program may use at most 128 MiB of HBM per device.

v0:
```python
import functools

import jax
import jax.numpy as jnp
from jax import lax
from jax.experimental import pallas as pl
from jax.experimental.pallas import tpu as pltpu
from jax.sharding import PartitionSpec as P

GW = 128
WIDTH = 2
MESH = pl.DeviceIdType.MESH


def smooth_grad(value):
    sigma = jax.nn.sigmoid(value)
    return sigma * (1.0 + value * (1.0 - sigma))


def fused_kernel(
    dims,
    states_ref,
    kernels_ref,
    feed_ref,
    final_ref,
    grads_ref,
    inbuf,
    outbuf,
    weights,
    taps,
    acc,
    gsend,
    gown,
    grecv,
    gout,
    in_sem,
    send_sem,
    weight_sem,
    final_sem,
    gsend_sem,
    grecv_sem,
    gout_sem,
):
    ticks, groups, images, height, width, share, shards = dims
    cells = height * width
    rows = images * cells
    pad = (height + 2) * width
    me = lax.axis_index("section")
    count = lax.axis_size("section")
    mine = lax.axis_index("dp")
    is_top = me == count - 1
    has_below = me > 0

    def lanes(group):
        start = group * GW
        return pl.ds(start if isinstance(group, int) else pl.multiple_of(start, GW), GW)

    def first_copy(group, stream):
        return pltpu.make_async_copy(
            states_ref.at[stream, :, lanes(group)],
            inbuf.at[0, group, stream],
            in_sem.at[0, group, stream],
        )

    def feed_copy(tick, group, stream):
        return pltpu.make_async_copy(
            feed_ref.at[tick - 1, stream, :, lanes(group)],
            inbuf.at[tick, group, stream],
            in_sem.at[tick, group, stream],
        )

    def weight_copy(group, branch):
        return pltpu.make_async_copy(
            kernels_ref.at[branch, :, lanes(group)],
            weights.at[branch, group],
            weight_sem.at[branch, group],
        )

    def final_copy(group, stream):
        return pltpu.make_async_copy(
            outbuf.at[ticks - 1, group, stream],
            final_ref.at[stream, :, lanes(group)],
            final_sem.at[group, stream],
        )

    def below_copy(tick, group, stream):
        return pltpu.make_async_remote_copy(
            src_ref=outbuf.at[tick, group, stream],
            dst_ref=inbuf.at[tick + 1, group, stream],
            send_sem=send_sem.at[tick, group, stream],
            recv_sem=in_sem.at[tick + 1, group, stream],
            device_id={"section": me - 1},
            device_id_type=MESH,
        )

    def share_copy(group, branch, offset):
        partner = lax.rem(mine + offset, shards)
        return pltpu.make_async_remote_copy(
            src_ref=gsend.at[branch, group, pl.ds(pl.multiple_of(partner * share, 16), share)],
            dst_ref=grecv.at[offset - 1, branch, group],
            send_sem=gsend_sem.at[offset - 1, branch, group],
            recv_sem=grecv_sem.at[offset - 1, branch, group],
            device_id={"dp": partner},
            device_id_type=MESH,
        )

    def gout_copy(group, branch):
        return pltpu.make_async_copy(
            gout.at[branch, group],
            grads_ref.at[branch, :, lanes(group)],
            gout_sem.at[branch, group],
        )

    for group in range(groups):
        for stream in range(4):
            first_copy(group, stream).start()
        for branch in range(2):
            weight_copy(group, branch).start()

    @pl.when(is_top)
    def _():
        @pl.loop(1, ticks)
        def _(tick):
            for group in range(groups):
                for stream in range(4):
                    feed_copy(tick, group, stream).start()

    barrier = pltpu.get_barrier_semaphore()

    @pl.when(has_below)
    def _():
        pl.semaphore_signal(barrier, inc=1, device_id={"section": me - 1}, device_id_type=MESH)

    @pl.when(jnp.logical_not(is_top))
    def _():
        pl.semaphore_signal(barrier, inc=1, device_id={"section": me + 1}, device_id_type=MESH)

    for offset in range(1, shards):
        pl.semaphore_signal(
            barrier,
            inc=1,
            device_id={"dp": lax.rem(mine + offset, shards)},
            device_id_type=MESH,
        )

    edge = jnp.zeros((4, images, width, 3 * GW), jnp.bfloat16)
    taps[:, :, 0:width, :] = edge
    taps[:, :, pad - width : pad, :] = edge
    acc[...] = jnp.zeros_like(acc)

    greeted = jnp.where(has_below, 1, 0) + jnp.where(is_top, 0, 1) + (shards - 1)
    pl.semaphore_wait(barrier, greeted)

    column = lax.rem(lax.broadcasted_iota(jnp.int32, (rows, GW), 0), width)
    at_left = column == 0
    at_right = column == width - 1

    def put_taps(slot, wide):
        left = jnp.where(at_left, 0.0, pltpu.roll(wide, 1, 0))
        right = jnp.where(at_right, 0.0, pltpu.roll(wide, rows - 1, 0))
        for place, piece in enumerate((left, wide, right)):
            taps[slot, :, width : width + cells, place * GW : (place + 1) * GW] = piece.astype(
                jnp.bfloat16
            ).reshape(images, cells, GW)

    def slab(slot):
        return jnp.concatenate(
            [
                taps[slot, :, row * width : row * width + cells, :].reshape(rows, 3 * GW)
                for row in range(3)
            ],
            axis=1,
        )

    def conv(slot, branch, group):
        return lax.dot_general(
            slab(slot),
            weights[branch, group],
            (((1,), (0,)), ((), ())),
            preferred_element_type=jnp.float32,
        )

    def conv_t(slot, branch, group):
        view = jnp.concatenate(
            [weights[branch, group, (8 - k) * GW : (9 - k) * GW, :] for k in range(9)], axis=1
        )
        return lax.dot_general(
            slab(slot),
            view,
            (((1,), (1,)), ((), ())),
            preferred_element_type=jnp.float32,
        )

    def add_term(branch, group, slot, grad):
        acc[branch, group] += lax.dot_general(
            grad,
            slab(slot),
            (((0,), (0,)), ((), ())),
            preferred_element_type=jnp.float32,
        )

    @pl.loop(0, ticks * groups)
    def _(step):
        inner = lax.rem(step, WIDTH * ticks)
        tick = inner // WIDTH
        group = (step // (WIDTH * ticks)) * WIDTH + lax.rem(inner, WIDTH)

        @pl.when(tick == 0)
        def _():
            for stream in range(4):
                first_copy(group, stream).wait()
            for branch in range(2):
                weight_copy(group, branch).wait()

        @pl.when(jnp.logical_and(tick > 0, is_top))
        def _():
            for stream in range(4):
                feed_copy(tick, group, stream).wait()

        @pl.when(jnp.logical_and(tick > 0, jnp.logical_not(is_top)))
        def _():
            for stream in range(4):
                below_copy(tick - 1, group, stream).wait_recv()

        def give(stream, value):
            outbuf[tick, group, stream] = value

            @pl.when(jnp.logical_and(tick < ticks - 1, has_below))
            def _():
                below_copy(tick, group, stream).start()

            @pl.when(tick == ticks - 1)
            def _():
                final_copy(group, stream).start()

        one = inbuf[tick, group, 0].astype(jnp.float32)
        grad_two = inbuf[tick, group, 3]
        put_taps(0, jax.nn.silu(one).astype(jnp.bfloat16).astype(jnp.float32))
        put_taps(1, grad_two.astype(jnp.float32))
        two = inbuf[tick, group, 1].astype(jnp.float32)
        input_two = (two - conv(0, 1, group)).astype(jnp.bfloat16)
        give(1, input_two)
        wide_two = input_two.astype(jnp.float32)
        put_taps(2, jax.nn.silu(wide_two).astype(jnp.bfloat16).astype(jnp.float32))
        total_one = (
            inbuf[tick, group, 2].astype(jnp.float32) + conv_t(1, 1, group) * smooth_grad(one)
        ).astype(jnp.bfloat16)
        give(2, total_one)
        put_taps(3, total_one.astype(jnp.float32))
        input_one = (one - conv(2, 0, group)).astype(jnp.bfloat16)
        give(0, input_one)
        total_two = (
            grad_two.astype(jnp.float32) + conv_t(3, 0, group) * smooth_grad(wide_two)
        ).astype(jnp.bfloat16)
        give(3, total_two)
        add_term(0, group, 2, total_one)
        add_term(1, group, 0, grad_two)

        @pl.when(tick == ticks - 1)
        def _():
            for branch in range(2):
                for k in range(9):
                    block = acc[branch, group, :, k * GW : (k + 1) * GW].T * (1.0 / cells)
                    gown[branch, group, k * GW : (k + 1) * GW, :] = block
                    gsend[branch, group, k * GW : (k + 1) * GW, :] = block.astype(jnp.bfloat16)
                for offset in range(1, shards):
                    share_copy(group, branch, offset).start()

    @pl.loop(0, groups)
    def _(group):
        for branch in range(2):
            total = gown[branch, group, pl.ds(pl.multiple_of(mine * share, 16), share), :]
            for offset in range(1, shards):
                share_copy(group, branch, offset).wait_recv()
                total = total + grecv[offset - 1, branch, group].astype(jnp.float32)
            gout[branch, group] = total
            gout_copy(group, branch).start()

    @pl.loop(0, groups)
    def _(group):
        for branch in range(2):
            gout_copy(group, branch).wait()
            for offset in range(1, shards):
                share_copy(group, branch, offset).wait_send()
        for stream in range(4):
            final_copy(group, stream).wait()

        @pl.when(has_below)
        def _():
            for tick in range(ticks - 1):
                for stream in range(4):
                    below_copy(tick, group, stream).wait_send()


def on_device(section_states, conv_kernels, top_feed):
    _, _, images, height, width, chans = section_states.shape
    ticks = top_feed.shape[0] + 1
    groups = chans // GW
    shards = lax.axis_size("dp")
    taps_rows = conv_kernels.shape[2]
    share = taps_rows // shards
    rows = images * height * width
    states = section_states.reshape(4, rows, chans)
    feed = top_feed.reshape(ticks - 1, 4, rows, chans)
    dims = (ticks, groups, images, height, width, share, shards)
    anywhere = pl.BlockSpec(memory_space=pl.ANY)
    dma = pltpu.SemaphoreType.DMA
    final, grads = pl.pallas_call(
        functools.partial(fused_kernel, dims),
        out_shape=(
            jax.ShapeDtypeStruct((4, rows, chans), jnp.bfloat16),
            jax.ShapeDtypeStruct((2, share, chans), jnp.float32),
        ),
        in_specs=[anywhere] * 3,
        out_specs=[anywhere] * 2,
        scratch_shapes=[
            pltpu.VMEM((ticks, groups, 4, rows, GW), jnp.bfloat16),
            pltpu.VMEM((ticks, groups, 4, rows, GW), jnp.bfloat16),
            pltpu.VMEM((2, groups, taps_rows, GW), jnp.bfloat16),
            pltpu.VMEM((4, images, (height + 2) * width, 3 * GW), jnp.bfloat16),
            pltpu.VMEM((2, groups, GW, taps_rows), jnp.float32),
            pltpu.VMEM((2, groups, taps_rows, GW), jnp.bfloat16),
            pltpu.VMEM((2, groups, taps_rows, GW), jnp.float32),
            pltpu.VMEM((max(shards - 1, 1), 2, groups, share, GW), jnp.bfloat16),
            pltpu.VMEM((2, groups, share, GW), jnp.float32),
            dma((ticks, groups, 4)),
            dma((ticks, groups, 4)),
            dma((2, groups)),
            dma((groups, 4)),
            dma((max(shards - 1, 1), 2, groups)),
            dma((max(shards - 1, 1), 2, groups)),
            dma((2, groups)),
        ],
        compiler_params=pltpu.CompilerParams(
            collective_id=0, has_side_effects=True, vmem_limit_bytes=56 * 1024 * 1024
        ),
    )(states, conv_kernels[0], feed)
    return (
        final.reshape(section_states.shape),
        grads.reshape(1, 2, share, chans),
    )


def solution(mesh):
    return jax.shard_map(
        on_device,
        mesh=mesh,
        in_specs=(
            P("section", None, "dp", None, None, None),
            P("section", None, None, None),
            P(None, None, "dp", None, None, None),
        ),
        out_specs=(P("section", None, "dp", None, None, None), P("section", None, "dp", None)),
        check_vma=False,
    )
```

profile of v0, /device:TPU:1, one launch (start us, length us, event | category | flops | bytes accessed | tf_op | source)
XLA Modules:
  0.0 63.0 jit_solution(9485535884756176290)
XLA Ops:
  0.6 56.8 %shard_map.50 = (bf16[4,256,512]{2,1,0:T(8,128)(2,1)}, f32[2,576,512]{2,1,0:T(8,128)}) custom-call(bf16[4,256,512]{2,1,0:T(8,128)(2,1)} %bitcast.10, bf16[2,1152,512]{2,1,0:T(8,128)(2,1)} %bitcast.8, bf16[3,4,256,512]{3,2,1,0:T(8,128)(2,1)} %bitcast.7), custom_call_target="tpu_custom_call" | custom-call | tf_op jit(solution)/shard_map/pallas_call | solution.py:308
  57.5 2.3 %copy.8 = bf16[1,4,1,16,16,512]{5,4,3,2,1,0:T(8,128)(2,1)} copy(bf16[1,4,1,16,16,512]{5,4,3,2,1,0:T(8,128)(2,1)} %bitcast.11) | data formatting | bytes 2097152
  59.7 3.3 %copy.9 = f32[1,2,576,512]{3,2,1,0:T(8,128)} copy(f32[1,2,576,512]{3,2,1,0:T(8,128)} %bitcast.9) | data formatting | bytes 4718592
where the time goes:
time: 63.2 us; the launch traced here: 63 us
  Pallas kernels  56.8 us (90%)
  local copies, waits for them, and re-layouts  5.54 us (9%)
  between operations  0.64 us (1%)
    pallas_call x1, Pallas kernels, on_device(): pl.pallas_call(functools.partial(fused_kernel, dims), out_shape=(jax.Shap...  56.8 us
    unnamed x2, local copies, waits for them, and re-layouts  5.54 us

commit v1 on v0

--- a/solution.py
+++ b/solution.py
@@ -8,13 +8,19 @@
 from jax.sharding import PartitionSpec as P
 
 GW = 128
-WIDTH = 2
 MESH = pl.DeviceIdType.MESH
 
 
 def smooth_grad(value):
     sigma = jax.nn.sigmoid(value)
     return sigma * (1.0 + value * (1.0 - sigma))
+
+
+def steps_in_order(groups, ticks):
+    tuned = ((0, 0), (1, 0), (2, 0), (0, 1), (1, 1), (0, 2), (2, 1), (1, 2), (0, 3), (3, 0), (2, 2), (1, 3), (3, 1), (2, 3), (3, 2), (3, 3))
+    if sorted(tuned) == [(group, tick) for group in range(groups) for tick in range(ticks)]:
+        return tuned
+    return [(group, tick) for tick in range(ticks) for group in range(groups)]
 
 
 def fused_kernel(
@@ -27,22 +33,21 @@
     inbuf,
     outbuf,
     weights,
+    flipped,
     taps,
     acc,
     gsend,
     gown,
     grecv,
-    gout,
     in_sem,
     send_sem,
     weight_sem,
-    final_sem,
     gsend_sem,
     grecv_sem,
-    gout_sem,
 ):
     ticks, groups, images, height, width, share, shards = dims
     cells = height * width
+    order = steps_in_order(groups, ticks)
     rows = images * cells
     pad = (height + 2) * width
     me = lax.axis_index("section")
@@ -74,13 +79,6 @@
             kernels_ref.at[branch, :, lanes(group)],
             weights.at[branch, group],
             weight_sem.at[branch, group],
-        )
-
-    def final_copy(group, stream):
-        return pltpu.make_async_copy(
-            outbuf.at[ticks - 1, group, stream],
-            final_ref.at[stream, :, lanes(group)],
-            final_sem.at[group, stream],
         )
 
     def below_copy(tick, group, stream):
@@ -104,13 +102,6 @@
             device_id_type=MESH,
         )
 
-    def gout_copy(group, branch):
-        return pltpu.make_async_copy(
-            gout.at[branch, group],
-            grads_ref.at[branch, :, lanes(group)],
-            gout_sem.at[branch, group],
-        )
-
     for group in range(groups):
         for stream in range(4):
             first_copy(group, stream).start()
@@ -149,8 +140,6 @@
     acc[...] = jnp.zeros_like(acc)
 
     greeted = jnp.where(has_below, 1, 0) + jnp.where(is_top, 0, 1) + (shards - 1)
-    pl.semaphore_wait(barrier, greeted)
-
     column = lax.rem(lax.broadcasted_iota(jnp.int32, (rows, GW), 0), width)
     at_left = column == 0
     at_right = column == width - 1
@@ -181,13 +170,10 @@
         )
 
     def conv_t(slot, branch, group):
-        view = jnp.concatenate(
-            [weights[branch, group, (8 - k) * GW : (9 - k) * GW, :] for k in range(9)], axis=1
-        )
         return lax.dot_general(
             slab(slot),
-            view,
-            (((1,), (1,)), ((), ())),
+            flipped[branch, group],
+            (((1,), (0,)), ((), ())),
             preferred_element_type=jnp.float32,
         )
 
@@ -201,9 +187,11 @@
 
     @pl.loop(0, ticks * groups)
     def _(step):
-        inner = lax.rem(step, WIDTH * ticks)
-        tick = inner // WIDTH
-        group = (step // (WIDTH * ticks)) * WIDTH + lax.rem(inner, WIDTH)
+        tick = jnp.int32(0)
+        group = jnp.int32(0)
+        for place, (at_group, at_tick) in enumerate(order):
+            tick = jnp.where(step == place, at_tick, tick)
+            group = jnp.where(step == place, at_group, group)
 
         @pl.when(tick == 0)
         def _():
@@ -211,6 +199,10 @@
                 first_copy(group, stream).wait()
             for branch in range(2):
                 weight_copy(group, branch).wait()
+                for k in range(9):
+                    flipped[branch, group, k * GW : (k + 1) * GW, :] = weights[
+                        branch, group, (8 - k) * GW : (9 - k) * GW, :
+                    ].T
 
         @pl.when(jnp.logical_and(tick > 0, is_top))
         def _():
@@ -231,7 +223,17 @@
 
             @pl.when(tick == ticks - 1)
             def _():
-                final_copy(group, stream).start()
+                final_ref[stream, :, lanes(group)] = value
+
+        def hand_on(branch):
+            @pl.when(tick == ticks - 1)
+            def _():
+                for k in range(9):
+                    block = acc[branch, group, :, k * GW : (k + 1) * GW].T * (1.0 / cells)
+                    gown[branch, group, k * GW : (k + 1) * GW, :] = block
+                    gsend[branch, group, k * GW : (k + 1) * GW, :] = block.astype(jnp.bfloat16)
+                for offset in range(1, shards):
+                    share_copy(group, branch, offset).start()
 
         one = inbuf[tick, group, 0].astype(jnp.float32)
         grad_two = inbuf[tick, group, 3]
@@ -239,7 +241,14 @@
         put_taps(1, grad_two.astype(jnp.float32))
         two = inbuf[tick, group, 1].astype(jnp.float32)
         input_two = (two - conv(0, 1, group)).astype(jnp.bfloat16)
+
+        @pl.when(step == 0)
+        def _():
+            pl.semaphore_wait(barrier, greeted)
+
         give(1, input_two)
+        add_term(1, group, 0, grad_two)
+        hand_on(1)
         wide_two = input_two.astype(jnp.float32)
         put_taps(2, jax.nn.silu(wide_two).astype(jnp.bfloat16).astype(jnp.float32))
         total_one = (
@@ -254,37 +263,22 @@
         ).astype(jnp.bfloat16)
         give(3, total_two)
         add_term(0, group, 2, total_one)
-        add_term(1, group, 0, grad_two)
-
-        @pl.when(tick == ticks - 1)
-        def _():
-            for branch in range(2):
-                for k in range(9):
-                    block = acc[branch, group, :, k * GW : (k + 1) * GW].T * (1.0 / cells)
-                    gown[branch, group, k * GW : (k + 1) * GW, :] = block
-                    gsend[branch, group, k * GW : (k + 1) * GW, :] = block.astype(jnp.bfloat16)
-                for offset in range(1, shards):
-                    share_copy(group, branch, offset).start()
+        hand_on(0)
 
     @pl.loop(0, groups)
     def _(group):
-        for branch in range(2):
+        for branch in (1, 0):
             total = gown[branch, group, pl.ds(pl.multiple_of(mine * share, 16), share), :]
             for offset in range(1, shards):
                 share_copy(group, branch, offset).wait_recv()
                 total = total + grecv[offset - 1, branch, group].astype(jnp.float32)
-            gout[branch, group] = total
-            gout_copy(group, branch).start()
+            grads_ref[branch, :, lanes(group)] = total
 
     @pl.loop(0, groups)
     def _(group):
         for branch in range(2):
-            gout_copy(group, branch).wait()
             for offset in range(1, shards):
                 share_copy(group, branch, offset).wait_send()
-        for stream in range(4):
-            final_copy(group, stream).wait()
-
         @pl.when(has_below)
         def _():
             for tick in range(ticks - 1):
@@ -303,33 +297,31 @@
     states = section_states.reshape(4, rows, chans)
     feed = top_feed.reshape(ticks - 1, 4, rows, chans)
     dims = (ticks, groups, images, height, width, share, shards)
-    anywhere = pl.BlockSpec(memory_space=pl.ANY)
+    anywhere = pl.BlockSpec(memory_space=pltpu.HBM)
     dma = pltpu.SemaphoreType.DMA
     final, grads = pl.pallas_call(
         functools.partial(fused_kernel, dims),
         out_shape=(
-            jax.ShapeDtypeStruct((4, rows, chans), jnp.bfloat16),
-            jax.ShapeDtypeStruct((2, share, chans), jnp.float32),
+            pltpu.VMEM((4, rows, chans), jnp.bfloat16),
+            pltpu.VMEM((2, share, chans), jnp.float32),
         ),
         in_specs=[anywhere] * 3,
-        out_specs=[anywhere] * 2,
+        out_specs=[pl.BlockSpec(memory_space=pltpu.VMEM)] * 2,
         scratch_shapes=[
             pltpu.VMEM((ticks, groups, 4, rows, GW), jnp.bfloat16),
             pltpu.VMEM((ticks, groups, 4, rows, GW), jnp.bfloat16),
+            pltpu.VMEM((2, groups, taps_rows, GW), jnp.bfloat16),
             pltpu.VMEM((2, groups, taps_rows, GW), jnp.bfloat16),
             pltpu.VMEM((4, images, (height + 2) * width, 3 * GW), jnp.bfloat16),
             pltpu.VMEM((2, groups, GW, taps_rows), jnp.float32),
             pltpu.VMEM((2, groups, taps_rows, GW), jnp.bfloat16),
             pltpu.VMEM((2, groups, taps_rows, GW), jnp.float32),
             pltpu.VMEM((max(shards - 1, 1), 2, groups, share, GW), jnp.bfloat16),
-            pltpu.VMEM((2, groups, share, GW), jnp.float32),
             dma((ticks, groups, 4)),
             dma((ticks, groups, 4)),
             dma((2, groups)),
-            dma((groups, 4)),
             dma((max(shards - 1, 1), 2, groups)),
             dma((max(shards - 1, 1), 2, groups)),
-            dma((2, groups)),
         ],
         compiler_params=pltpu.CompilerParams(
             collective_id=0, has_side_effects=True, vmem_limit_bytes=56 * 1024 * 1024

time: 63.2 us -> 54.4 us (0.86)
  Pallas kernels: 56.8 us -> 51.2 us
  local copies, waits for them, and re-layouts: 5.54 us -> 2.38 us
    pallas_call x1, Pallas kernels: 56.8 us -> 51.2 us  [on_device(): pl.pallas_call(functools.partial(fused_kernel, dims), out_shape=(pltpu.VM...]
    unnamed x2, local copies, waits for them, and re-layouts: 5.54 us -> 2.38 us
where the time goes in v1:
time: 54.4 us; the launch traced here: 54.2 us
  Pallas kernels  51.2 us (94%)
  local copies, waits for them, and re-layouts  2.38 us (4%)
  between operations  0.64 us (1%)
    pallas_call x1, Pallas kernels, on_device(): pl.pallas_call(functools.partial(fused_kernel, dims), out_shape=(pltpu.VM...  51.2 us
    unnamed x2, local copies, waits for them, and re-layouts  2.38 us

profile of v1, /device:TPU:1, one launch (start us, length us, event | category | flops | bytes accessed | tf_op | source)
XLA Modules:
  0.0 54.2 jit_solution(10303151648400891501)
XLA Ops:
  0.6 51.2 %shard_map.50 = (bf16[4,256,512]{2,1,0:T(8,128)(2,1)S(1)}, f32[2,576,512]{2,1,0:T(8,128)S(1)}) custom-call(bf16[4,256,512]{2,1,0:T(8,128)(2,1)} %bitcast.11, bf16[2,1152,512]{2,1,0:T(8,128)(2,1)} %bitcast.10, bf16[3,4,256,512]{3,2,1,0:T(8,128)(2,1)} %bitcast.9), custom_call_target="tpu_custom_call" | custom-call | tf_op jit(solution)/shard_map/pallas_call | solution.py:302
  51.8 1.0 %copy.8 = bf16[1,4,1,16,16,512]{5,4,3,2,1,0:T(8,128)(2,1)} copy(bf16[1,4,1,16,16,512]{5,4,3,2,1,0:T(8,128)(2,1)S(1)} %bitcast.8) | data formatting | bytes 2097152
  52.8 1.4 %copy.9 = f32[1,2,576,512]{3,2,1,0:T(8,128)} copy(f32[1,2,576,512]{3,2,1,0:T(8,128)S(1)} %bitcast.7) | data formatting | bytes 4718592

commit v2 on v1

--- a/solution.py
+++ b/solution.py
@@ -17,7 +17,7 @@
 
 
 def steps_in_order(groups, ticks):
-    tuned = ((0, 0), (1, 0), (2, 0), (0, 1), (1, 1), (0, 2), (2, 1), (1, 2), (0, 3), (3, 0), (2, 2), (1, 3), (3, 1), (2, 3), (3, 2), (3, 3))
+    tuned = ((0, 0), (1, 0), (0, 1), (2, 0), (0, 2), (1, 1), (0, 3), (2, 1), (1, 2), (3, 0), (1, 3), (2, 2), (3, 1), (2, 3), (3, 2), (3, 3))
     if sorted(tuned) == [(group, tick) for group in range(groups) for tick in range(ticks)]:
         return tuned
     return [(group, tick) for tick in range(ticks) for group in range(groups)]
@@ -48,6 +48,7 @@
     ticks, groups, images, height, width, share, shards = dims
     cells = height * width
     order = steps_in_order(groups, ticks)
+    sends = ((1, 2), (0, 1), (3, 1))
     rows = images * cells
     pad = (height + 2) * width
     me = lax.axis_index("section")
@@ -81,10 +82,10 @@
             weight_sem.at[branch, group],
         )
 
-    def below_copy(tick, group, stream):
+    def below_copy(tick, group, stream, size):
         return pltpu.make_async_remote_copy(
-            src_ref=outbuf.at[tick, group, stream],
-            dst_ref=inbuf.at[tick + 1, group, stream],
+            src_ref=outbuf.at[tick, group, pl.ds(stream, size)],
+            dst_ref=inbuf.at[tick + 1, group, pl.ds(stream, size)],
             send_sem=send_sem.at[tick, group, stream],
             recv_sem=in_sem.at[tick + 1, group, stream],
             device_id={"section": me - 1},
@@ -187,11 +188,15 @@
 
     @pl.loop(0, ticks * groups)
     def _(step):
-        tick = jnp.int32(0)
-        group = jnp.int32(0)
-        for place, (at_group, at_tick) in enumerate(order):
-            tick = jnp.where(step == place, at_tick, tick)
-            group = jnp.where(step == place, at_group, group)
+        word = jnp.int32(0)
+        for place in range(0, len(order), 3):
+            packed = 0
+            for at, (at_group, at_tick) in enumerate(order[place : place + 3]):
+                packed |= (at_group * 32 + at_tick) << (10 * at)
+            word = jnp.where(step >= place, packed, word)
+        entry = lax.shift_right_logical(word, 10 * lax.rem(step, 3))
+        tick = entry & 31
+        group = lax.shift_right_logical(entry, 5) & 31
 
         @pl.when(tick == 0)
         def _():
@@ -211,19 +216,18 @@
 
         @pl.when(jnp.logical_and(tick > 0, jnp.logical_not(is_top)))
         def _():
-            for stream in range(4):
-                below_copy(tick - 1, group, stream).wait_recv()
-
-        def give(stream, value):
-            outbuf[tick, group, stream] = value
-
+            for stream, size in sends:
+                below_copy(tick - 1, group, stream, size).wait_recv()
+
+        def give(first, size):
             @pl.when(jnp.logical_and(tick < ticks - 1, has_below))
             def _():
-                below_copy(tick, group, stream).start()
+                below_copy(tick, group, first, size).start()
 
             @pl.when(tick == ticks - 1)
             def _():
-                final_ref[stream, :, lanes(group)] = value
+                for stream in range(first, first + size):
+                    final_ref[stream, :, lanes(group)] = outbuf[tick, group, stream]
 
         def hand_on(branch):
             @pl.when(tick == ticks - 1)
@@ -241,28 +245,31 @@
         put_taps(1, grad_two.astype(jnp.float32))
         two = inbuf[tick, group, 1].astype(jnp.float32)
         input_two = (two - conv(0, 1, group)).astype(jnp.bfloat16)
-
-        @pl.when(step == 0)
-        def _():
-            pl.semaphore_wait(barrier, greeted)
-
-        give(1, input_two)
-        add_term(1, group, 0, grad_two)
-        hand_on(1)
-        wide_two = input_two.astype(jnp.float32)
-        put_taps(2, jax.nn.silu(wide_two).astype(jnp.bfloat16).astype(jnp.float32))
+        outbuf[tick, group, 1] = input_two
+        put_taps(2, jax.nn.silu(input_two.astype(jnp.float32)).astype(jnp.bfloat16).astype(jnp.float32))
         total_one = (
             inbuf[tick, group, 2].astype(jnp.float32) + conv_t(1, 1, group) * smooth_grad(one)
         ).astype(jnp.bfloat16)
-        give(2, total_one)
+        outbuf[tick, group, 2] = total_one
         put_taps(3, total_one.astype(jnp.float32))
-        input_one = (one - conv(2, 0, group)).astype(jnp.bfloat16)
-        give(0, input_one)
-        total_two = (
-            grad_two.astype(jnp.float32) + conv_t(3, 0, group) * smooth_grad(wide_two)
+        add_term(1, group, 0, inbuf[tick, group, 3])
+
+        @pl.when(step == 0)
+        def _():
+            pl.semaphore_wait(barrier, greeted)
+
+        give(1, 2)
+        hand_on(1)
+        outbuf[tick, group, 0] = (
+            inbuf[tick, group, 0].astype(jnp.float32) - conv(2, 0, group)
         ).astype(jnp.bfloat16)
-        give(3, total_two)
-        add_term(0, group, 2, total_one)
+        outbuf[tick, group, 3] = (
+            inbuf[tick, group, 3].astype(jnp.float32)
+            + conv_t(3, 0, group) * smooth_grad(outbuf[tick, group, 1].astype(jnp.float32))
+        ).astype(jnp.bfloat16)
+        give(0, 1)
+        give(3, 1)
+        add_term(0, group, 2, outbuf[tick, group, 2])
         hand_on(0)
 
     @pl.loop(0, groups)
@@ -282,8 +289,8 @@
         @pl.when(has_below)
         def _():
             for tick in range(ticks - 1):
-                for stream in range(4):
-                    below_copy(tick, group, stream).wait_send()
+                for stream, size in sends:
+                    below_copy(tick, group, stream, size).wait_send()
 
 
 def on_device(section_states, conv_kernels, top_feed):

time: 54.4 us -> 53.8 us (0.989)
  Pallas kernels: 51.2 us -> 50.6 us
    pallas_call x1, Pallas kernels: 51.2 us -> 50.6 us  [on_device(): pl.pallas_call(functools.partial(fused_kernel, dims), out_shape=(pltpu.VM...]
where the time goes in v2:
time: 53.8 us; the launch traced here: 53.6 us
  Pallas kernels  50.6 us (94%)
  local copies, waits for them, and re-layouts  2.38 us (4%)
  between operations  0.64 us (1%)
    pallas_call x1, Pallas kernels, on_device(): pl.pallas_call(functools.partial(fused_kernel, dims), out_shape=(pltpu.VM...  50.6 us
    unnamed x2, local copies, waits for them, and re-layouts  2.38 us

profile of v2, /device:TPU:1, one launch (start us, length us, event | category | flops | bytes accessed | tf_op | source)
XLA Modules:
  0.0 53.6 jit_solution(2610412273734577233)
XLA Ops:
  0.6 50.6 %shard_map.50 = (bf16[4,256,512]{2,1,0:T(8,128)(2,1)S(1)}, f32[2,576,512]{2,1,0:T(8,128)S(1)}) custom-call(bf16[4,256,512]{2,1,0:T(8,128)(2,1)} %bitcast.11, bf16[2,1152,512]{2,1,0:T(8,128)(2,1)} %bitcast.10, bf16[3,4,256,512]{3,2,1,0:T(8,128)(2,1)} %bitcast.9), custom_call_target="tpu_custom_call" | custom-call | tf_op jit(solution)/shard_map/pallas_call | solution.py:309
  51.2 1.0 %copy.8 = bf16[1,4,1,16,16,512]{5,4,3,2,1,0:T(8,128)(2,1)} copy(bf16[1,4,1,16,16,512]{5,4,3,2,1,0:T(8,128)(2,1)S(1)} %bitcast.8) | data formatting | bytes 2097152
  52.2 1.4 %copy.9 = f32[1,2,576,512]{3,2,1,0:T(8,128)} copy(f32[1,2,576,512]{3,2,1,0:T(8,128)S(1)} %bitcast.7) | data formatting | bytes 4718592
